TPU v7x, 128 devices: a whole 4x4x4 slice. The times are simulated.
128 devices in a mesh: expert: 4 (over z), seq: 4 (over y), tensor: 8 (over x, core).
Axes of the slice: x: 4, y: 4, z: 4, core: 2. Of those that a mesh axis runs over, the one named last changes fastest.
Arguments:
- tokens: bfloat16 [3072, 7168], P(('expert', 'seq')), may hold values from -6 to 6
- grad_out: bfloat16 [3072, 7168], P(('expert', 'seq')), may hold values from -6 to 6
- expert_ids: int32 [3072, 2], P(('expert', 'seq')), may hold values from 0 to 3, all different within a row; in each aligned block of 192 rows (0 to 191, 192 to 383, ...) at most 128 rows name the same one
- route_weights: bfloat16 [3072, 2], P(('expert', 'seq')), may hold values from 0.099609375 to 1
- gate_weight: bfloat16 [4, 7168, 2048], P('expert', 'seq', 'tensor'), may hold values from -0.0625 to 0.0625
- up_weight: bfloat16 [4, 7168, 2048], P('expert', 'seq', 'tensor'), may hold values from -0.0625 to 0.0625
- down_weight: bfloat16 [4, 7168, 2048], P('expert', 'seq', 'tensor'), may hold values from -0.125 to 0.125
Outputs:
- grad_tokens: bfloat16 [3072, 7168], P(('expert', 'seq'), 'tensor')
- grad_route: float32 [3072, 2], P(('expert', 'seq'))
- grad_gate: float32 [4, 7168, 2048], P('expert', 'seq', 'tensor')
- grad_up: float32 [4, 7168, 2048], P('expert', 'seq', 'tensor')
- grad_down: float32 [4, 7168, 2048], P('expert', 'seq', 'tensor')
Inputs may be any that keep to these rules, and one draw needn't show every extreme that they name: `expert_ids`: the two ids of a row differ. Within each aligned block of 192 rows (the tokens of one group of the expert and seq axes) no expert is named by more than 128 rows, and in some block an expert is named by exactly 128 rows.
All inputs are finite; a program needn't handle non-finite values.
Results may differ from a plain program's by a relative error of at most 0.019.
Values may be sent and summed in bfloat16 or wider, within the bound.
A program may use at most 192 MiB of HBM per device.

v0:
```python
import jax
import jax.numpy as jnp
from jax import lax
from jax.sharding import PartitionSpec as P


def shards(tokens, grad_out, expert_ids, route_weights, gate_weight, up_weight, down_weight):
    expert_count = lax.axis_size("expert")
    seq_count = lax.axis_size("seq")
    tensor_count = lax.axis_size("tx") * lax.axis_size("core")
    core = lax.axis_index("core")
    local_count = gate_weight.shape[0]
    tok_rows = tokens.shape[0]
    model_width = tokens.shape[1]
    part_width = model_width // tensor_count
    per_peer = tok_rows // 6
    peer_count = expert_count * seq_count
    block_rows = local_count * per_peer
    slot_count = peer_count * block_rows
    flat_ids = expert_ids.reshape(-1)
    route_count = flat_ids.shape[0]
    onehot = (
        flat_ids[:, None] == jnp.arange(local_count * expert_count, dtype=jnp.int32)[None, :]
    ).astype(jnp.int32)
    before = jnp.cumsum(onehot, axis=0) - onehot
    ranking = jnp.sum(before * onehot, axis=1)
    local_expert = flat_ids % local_count
    dest_peer = flat_ids // local_count * seq_count + ranking % seq_count
    target = (dest_peer * local_count + local_expert) * per_peer + ranking // seq_count
    source = (
        jnp.full((slot_count,), -1, jnp.int32)
        .at[target]
        .set(jnp.arange(route_count, dtype=jnp.int32))
    )
    filled = source >= 0
    safe_source = jnp.maximum(source, 0)
    token_of = safe_source // 2
    keep = filled[:, None].astype(tokens.dtype)
    weight_send = (
        route_weights.reshape(-1)[safe_source] * filled.astype(route_weights.dtype)
    ).reshape(peer_count, block_rows)
    half = model_width // 2
    tokens_half = lax.dynamic_slice_in_dim(tokens, core * half, half, axis=1)
    grad_half = lax.dynamic_slice_in_dim(grad_out, core * half, half, axis=1)
    in_send = (tokens_half[token_of] * keep).reshape(peer_count, block_rows, half)
    out_send = (grad_half[token_of] * keep).reshape(peer_count, block_rows, half)
    in_mine, out_mine, weight_recv = (
        lax.all_to_all(in_send, ("expert", "seq"), split_axis=0, concat_axis=0, tiled=True),
        lax.all_to_all(out_send, ("expert", "seq"), split_axis=0, concat_axis=0, tiled=True),
        lax.all_to_all(weight_send, ("expert", "seq"), split_axis=0, concat_axis=0, tiled=True),
    )

    def join_halves(mine):
        other = lax.ppermute(mine, "core", [(0, 1), (1, 0)])
        first = jnp.where(core == 0, mine, other)
        second = jnp.where(core == 0, other, mine)
        return jnp.concatenate([first, second], axis=-1)

    in_recv = join_halves(in_mine)
    out_recv = join_halves(out_mine)

    def by_expert(values):
        shaped = values.reshape((peer_count, local_count, per_peer) + values.shape[2:])
        return jnp.swapaxes(shaped, 0, 1).reshape(
            (local_count, peer_count * per_peer) + values.shape[2:]
        )

    def by_peer(values):
        shaped = values.reshape((local_count, peer_count, per_peer) + values.shape[2:])
        return jnp.swapaxes(shaped, 0, 1).reshape((peer_count, block_rows) + values.shape[2:])

    in_rows = by_expert(in_recv)
    out_rows = by_expert(out_recv)
    prob = by_expert(weight_recv).astype(jnp.float32)[:, :, None]
    gate_full, up_full, down_full = (
        lax.all_gather(gate_weight, "seq", axis=1, tiled=True),
        lax.all_gather(up_weight, "seq", axis=1, tiled=True),
        lax.all_gather(down_weight, "seq", axis=1, tiled=True),
    )
    pre_gate = jnp.einsum("emd,edf->emf", in_rows, gate_full, preferred_element_type=jnp.float32)
    pre_up = jnp.einsum("emd,edf->emf", in_rows, up_full, preferred_element_type=jnp.float32)
    sigmoid_gate = jax.nn.sigmoid(pre_gate)
    silu_gate = pre_gate * sigmoid_gate
    hidden = silu_gate * pre_up
    hidden_low = hidden.astype(jnp.bfloat16)
    back_proj = jnp.einsum("emd,edf->emf", out_rows, down_full, preferred_element_type=jnp.float32)
    partial_scores = jnp.sum(hidden * back_proj, axis=2)
    scaled = (prob * out_rows.astype(jnp.float32)).astype(jnp.bfloat16)
    hidden_grad = prob * back_proj
    up_grad = (hidden_grad * silu_gate).astype(jnp.bfloat16)
    gate_grad = (
        hidden_grad * pre_up * sigmoid_gate * (1.0 + pre_gate * (1.0 - sigmoid_gate))
    ).astype(jnp.bfloat16)
    input_terms = jnp.einsum(
        "emf,edf->emd", gate_grad, gate_full, preferred_element_type=jnp.float32
    )
    input_terms = input_terms + jnp.einsum(
        "emf,edf->emd", up_grad, up_full, preferred_element_type=jnp.float32
    )
    route_scores = lax.psum(partial_scores, ("tx", "core"))
    input_shards = lax.psum_scatter(
        input_terms.astype(jnp.bfloat16), ("tx", "core"), scatter_dimension=2, tiled=True
    ).astype(jnp.float32)
    back_rows, back_scores = (
        lax.all_to_all(
            by_peer(input_shards).astype(jnp.bfloat16),
            ("expert", "seq"),
            split_axis=0,
            concat_axis=0,
            tiled=True,
        ).astype(jnp.float32),
        lax.all_to_all(
            by_peer(route_scores).astype(jnp.bfloat16),
            ("expert", "seq"),
            split_axis=0,
            concat_axis=0,
            tiled=True,
        ).astype(jnp.float32),
    )
    route_rows = back_rows.reshape(slot_count, part_width)[target].reshape(tok_rows, 2, part_width)
    grad_tokens = jnp.sum(route_rows, axis=1).astype(jnp.bfloat16)
    grad_route = back_scores.reshape(slot_count)[target].reshape(tok_rows, 2)
    gate_part = jnp.einsum("emd,emf->edf", in_rows, gate_grad, preferred_element_type=jnp.float32)
    up_part = jnp.einsum("emd,emf->edf", in_rows, up_grad, preferred_element_type=jnp.float32)
    down_part = jnp.einsum("emd,emf->edf", scaled, hidden_low, preferred_element_type=jnp.float32)
    grad_gate, grad_up, grad_down = (
        lax.psum_scatter(
            gate_part.astype(jnp.bfloat16), "seq", scatter_dimension=1, tiled=True
        ).astype(jnp.float32),
        lax.psum_scatter(
            up_part.astype(jnp.bfloat16), "seq", scatter_dimension=1, tiled=True
        ).astype(jnp.float32),
        lax.psum_scatter(
            down_part.astype(jnp.bfloat16), "seq", scatter_dimension=1, tiled=True
        ).astype(jnp.float32),
    )
    return (grad_tokens, grad_route, grad_gate, grad_up, grad_down)


def solution(mesh):
    shape = mesh.devices.shape
    mesh = jax.sharding.Mesh(
        mesh.devices.reshape(shape[0], shape[1], shape[2] // 2, 2), ("expert", "seq", "tx", "core")
    )
    tensor = ("tx", "core")
    placed = (
        P(("expert", "seq"), None),
        P(("expert", "seq"), None),
        P(("expert", "seq"), None),
        P(("expert", "seq"), None),
        P("expert", "seq", tensor),
        P("expert", "seq", tensor),
        P("expert", "seq", tensor),
    )
    return jax.shard_map(
        shards,
        mesh=mesh,
        in_specs=placed,
        out_specs=(
            P(("expert", "seq"), tensor),
            P(("expert", "seq"), None),
            P("expert", "seq", tensor),
            P("expert", "seq", tensor),
            P("expert", "seq", tensor),
        ),
        check_vma=False,
    )
```

profile of v0, /device:TPU:1, one launch (start us, length us, event | category | flops | bytes accessed | tf_op | source)
XLA Modules:
  0.0 511.5 jit_solution(3057996658511665825)
XLA Ops:
  7.2 0.7 all-gather.8.cloned.1.call-update
  7.9 0.8 copy.24
  8.7 0.1 eq.38
  8.8 0.1 eq.34
  9.0 0.8 copy.26
  9.8 0.2 reshape.290
  10.0 0.7 broadcast_multiply_fusion.2
  10.7 0.1 copy.23
  10.8 0.1 mul.119
  11.0 1.2 reduce-window.6
  12.2 0.2 slice_reduce_fusion
  12.4 0.2 reduce-window.9
  12.7 2.9 scatter_custom_fusion
  15.7 3.5 gather_fusion
  19.2 0.1 reshape.301
  19.3 1.9 constant_dynamic-slice_fusion
  21.2 4.2 gather_fusion.2
  25.4 4.2 gather_fusion.1
  29.6 6.8 %broadcast_multiply_fusion.1 = (bf16[16,32,3584]{2,1,0:T(8,128)(2,1)}, bf16[16,32,3584]{2,1,0:T(8,128)(2,1)}) fusion(bf16[16,32,3584]{2,1,0:T(8,128)(2,1)} %bitcast.74, bf16[16,32]{1,0:T(8,128)(2,1)S(1)} %reshape.301, bf16[16,32,3584]{2,1,0:T(8,128)(2,1)} %bitcast.73), kind=kLoop, calls=%fused_computation.34 | loop fusion | flops 3670016 | bytes 14681088 | tf_op jit(solution)/shard_map/mul | solution.py:46
  36.4 8.9 %all-to-all-start.2 = ((bf16[16,32,3584]{2,1,0:T(8,128)(2,1)}), bf16[16,32,3584]{2,1,0:T(8,128)(2,1)}, u32[]{:S(2)}, u32[]{:S(2)}) async-start(bf16[16,32,3584]{2,1,0:T(8,128)(2,1)} %get-tuple-element.30), calls=%async_computation.2 | async-start | bytes 7340032 | tf_op jit(solution)/shard_map/all_to_all | solution.py:48
  45.3 0.7 all-gather.6.cloned.1.call-update
  46.0 70.6 %all-to-all-done.2 = bf16[16,32,3584]{2,1,0:T(8,128)(2,1)} async-done(((bf16[16,32,3584]{2,1,0:T(8,128)(2,1)}), bf16[16,32,3584]{2,1,0:T(8,128)(2,1)}, u32[]{:S(2)}, u32[]{:S(2)}) %all-to-all-start.2) | async-done | bytes 3670048 | tf_op jit(solution)/shard_map/all_to_all | solution.py:48
  116.7 1.8 collective-permute-start.1
  118.5 0.1 all_to_all.25
  118.6 11.5 %all_to_all.31 = bf16[16,1,32]{2,1,0:T(2,128)(2,1)S(1)} all-to-all(bf16[16,1,32]{2,1,0:T(2,128)(2,1)S(1)} %all_to_all.25), channel_id=1, replica_groups=mesh['expert'=4,'seq'=4,'tx'=4,'core'=2] {'expert','seq'}, dimensions={0} | all-to-all | bytes 2048 | tf_op jit(solution)/shard_map/all_to_all | solution.py:50
  130.1 4.5 all-to-all-start.1
  134.7 0.7 all-gather.4.cloned.1.call-update
  135.4 0.1 reshape.300
  135.5 64.9 %all-to-all-done.1 = bf16[16,32,3584]{2,1,0:T(8,128)(2,1)} async-done(((bf16[16,32,3584]{2,1,0:T(8,128)(2,1)}), bf16[16,32,3584]{2,1,0:T(8,128)(2,1)}, u32[]{:S(2)}, u32[]{:S(2)}) %all-to-all-start.1) | async-done | bytes 3670048 | tf_op jit(solution)/shard_map/all_to_all | solution.py:49
  200.5 6.6 %collective-permute-start = (bf16[16,32,3584]{2,1,0:T(8,128)(2,1)}, bf16[16,32,3584]{2,1,0:T(8,128)(2,1)}, u32[]{:S(2)}, u32[]{:S(2)}) collective-permute-start(bf16[16,32,3584]{2,1,0:T(8,128)(2,1)} %all-to-all-done.1), channel_id=1, source_target_pairs={{0,1},{1,0},{2,3},{3,2},{4,5},{5,4},{6,7},{7,6},{8,9},{9,8},{10,11... | collective-permute-start | bytes 11010056 | tf_op jit(solution)/shard_map/ppermute | solution.py:54
  207.0 5.4 %broadcast_select_fusion.1 = (bf16[16,32,3584]{2,1,0:T(8,128)(2,1)S(1)}, bf16[16,32,3584]{2,1,0:T(8,128)(2,1)}) fusion(bf16[16,32,3584]{2,1,0:T(8,128)(2,1)} %all-to-all-done.2, bf16[16,32,3584]{2,1,0:T(8,128)(2,1)} %collective-permute-done.1, pred[]{:T(512)S(6)} %eq.42), kind=kLoop, calls=%fused_computation.29 | loop fusion | flops 3670016 | bytes 14680065 | tf_op jit(solution)/shard_map/jit(_where)/select_n | solution.py:55
  212.5 5.8 %pad_maximum_fusion.1 = bf16[16,32,7168]{2,1,0:T(8,128)(2,1)} fusion(bf16[16,32,3584]{2,1,0:T(8,128)(2,1)} %get-tuple-element.25, bf16[16,32,3584]{2,1,0:T(8,128)(2,1)S(1)} %get-tuple-element.24), kind=kLoop, calls=%fused_computation.16 | loop fusion | flops 14680064 | bytes 14680064 | tf_op jit(solution)/shard_map/concatenate | solution.py:57
  218.2 6.2 %fusion.7 = f32[512,256]{0,1:T(8,128)S(1)} fusion(bf16[512,7168]{1,0:T(8,128)(2,1)} %bitcast.67, bf16[1,7168,256]{2,1,0:T(8,128)(2,1)} %all-gather.8.cloned.1.call-done), kind=kOutput, calls=%fused_computation.21 | convolution fusion | flops 1879048192 | bytes 11534336 | tf_op jit(solution)/shard_map/emd,edf->emf/dot_general | solution.py:80
  224.5 6.2 %fusion.10 = f32[512,256]{0,1:T(8,128)S(1)} fusion(bf16[512,7168]{1,0:T(8,128)(2,1)} %bitcast.68, bf16[1,7168,256]{2,1,0:T(8,128)(2,1)} %all-gather.6.cloned.1.call-done), kind=kOutput, calls=%fused_computation.24 | convolution fusion | flops 1879048192 | bytes 11534336 | tf_op jit(solution)/shard_map/emd,edf->emf/dot_general | solution.py:81
  230.7 5.6 %broadcast_select_fusion.3 = (bf16[16,32,3584]{2,1,0:T(8,128)(2,1)S(1)}, bf16[16,32,3584]{2,1,0:T(8,128)(2,1)}) fusion(bf16[16,32,3584]{2,1,0:T(8,128)(2,1)} %all-to-all-done.1, bf16[16,32,3584]{2,1,0:T(8,128)(2,1)} %collective-permute-done, pred[]{:T(512)S(6)} %eq.42), kind=kLoop, calls=%fused_computation.31 | loop fusion | flops 3670016 | bytes 14680065 | tf_op jit(solution)/shard_map/jit(_where)/select_n | solution.py:55
  236.3 5.8 %pad_maximum_fusion = bf16[16,32,7168]{2,1,0:T(8,128)(2,1)} fusion(bf16[16,32,3584]{2,1,0:T(8,128)(2,1)} %get-tuple-element.23, bf16[16,32,3584]{2,1,0:T(8,128)(2,1)S(1)} %get-tuple-element.22), kind=kLoop, calls=%fused_computation.15 | loop fusion | flops 14680064 | bytes 14680064 | tf_op jit(solution)/shard_map/concatenate | solution.py:57
  242.1 6.6 %multiply_reduce_fusion = (f32[512]{0:T(512)S(1)}, bf16[512,256]{0,1:T(8,128)(2,1)S(1)}, bf16[512,256]{0,1:T(8,128)(2,1)S(1)}) fusion(f32[512,256]{0,1:T(8,128)S(1)} %fusion.10, f32[512,256]{0,1:T(8,128)S(1)} %fusion.7, f32[512]{0:T(512)S(1)} %reshape.300, bf16[512,7168]{1,0:T(8,128)(2,1)} %bitcast.75, bf16[1,7168,256]{2,1,0:T(8,128)(2,1)} %all-gather.4.cloned.1.call-done), kind=kOutput, calls=%fused_computation.36 | convolution fusion | flops 1881275904 | bytes 12587008 | tf_op jit(solution)/shard_map/emd,edf->emf/dot_general | solution.py:86
  248.7 7.3 %fusion.5 = f32[512,7168]{1,0:T(8,128)} fusion(bf16[512,256]{0,1:T(8,128)(2,1)S(1)} %get-tuple-element.27, bf16[1,7168,256]{2,1,0:T(8,128)(2,1)S(1)} %copy-done.1), kind=kOutput, calls=%fused_computation.19 | convolution fusion | flops 1879048192 | bytes 18612224 | tf_op jit(solution)/shard_map/emf,edf->emd/dot_general | solution.py:94
  256.0 10.6 %fusion = bf16[1,512,7168]{2,1,0:T(8,128)(2,1)} fusion(f32[512,7168]{1,0:T(8,128)} %fusion.5, bf16[512,256]{0,1:T(8,128)(2,1)S(1)} %get-tuple-element.28, bf16[1,7168,256]{2,1,0:T(8,128)(2,1)S(1)} %copy-done), kind=kOutput, calls=%fused_computation.8 | convolution fusion | flops 1886388224 | bytes 25952256 | tf_op jit(solution)/shard_map/emf,edf->emd/dot_general | solution.py:97
  266.6 31.4 %copy.30 = bf16[1,512,7168]{1,0,2:T(2,128)(2,1)} copy(bf16[1,512,7168]{2,1,0:T(8,128)(2,1)} %fusion) | data formatting | bytes 14680064
  298.1 10.3 %copy.36 = bf16[7168,1,512]{2,0,1:T(8,128)(2,1)} copy(bf16[7168,1,512]{2,1,0:T(2,128)(2,1)} %bitcast.71) | data formatting | bytes 14680064
  308.5 8.0 %fusion.3 = bf16[1,7168,256]{2,1,0:T(8,128)(2,1)} fusion(bf16[512,7168]{1,0:T(8,128)(2,1)} %bitcast.76, f32[512]{0:T(512)S(1)} %reshape.300, f32[512,256]{0,1:T(8,128)S(1)} %fusion.10, f32[512,256]{0,1:T(8,128)S(1)} %fusion.7), kind=kOutput, calls=%fused_computation.14 | convolution fusion | flops 1892679680 | bytes 12060672 | tf_op jit(solution)/shard_map/emd,emf->edf/dot_general | solution.py:125
  316.6 7.1 %fusion.1 = bf16[1,7168,256]{2,1,0:T(8,128)(2,1)} fusion(bf16[512,7168]{1,0:T(8,128)(2,1)} %bitcast.69, bf16[512,256]{0,1:T(8,128)(2,1)S(1)} %get-tuple-element.27), kind=kOutput, calls=%fused_computation.12 | convolution fusion | flops 1880883200 | bytes 11272192 | tf_op jit(solution)/shard_map/emd,emf->edf/dot_general | solution.py:123
  323.8 7.2 %fusion.2 = bf16[1,7168,256]{2,1,0:T(8,128)(2,1)} fusion(bf16[512,7168]{1,0:T(8,128)(2,1)} %bitcast.70, bf16[512,256]{0,1:T(8,128)(2,1)S(1)} %get-tuple-element.28), kind=kOutput, calls=%fused_computation.13 | convolution fusion | flops 1880883200 | bytes 11272192 | tf_op jit(solution)/shard_map/emd,emf->edf/dot_general | solution.py:124
  330.9 23.5 %psum.7 = bf16[1,512]{1,0:T(2,128)(2,1)S(1)} all-reduce(f32[1,512]{1,0:T(1,128)S(1)} %bitcast.78), channel_id=1, replica_groups=mesh['expert'=4,'seq'=4,'tx'=4,'core'=2] {'tx','core'}, use_global_device_ids=true, to_apply=%region_7.8 | all-reduce | flops 512 | bytes 3072 | tf_op jit(solution)/shard_map/psum | solution.py:100
  354.4 0.7 convert_element_type.144
  355.1 3.7 all-to-all-start.4
  358.9 2.1 reshape_bitcast_fusion
  361.0 3.4 copy.31
  364.4 0.7 all-to-all-done.4
  365.1 6.0 %all-to-all-start.3 = ((bf16[16,32,896]{2,1,0:T(8,128)(2,1)}), bf16[16,32,896]{2,1,0:T(8,128)(2,1)S(1)}, u32[]{:S(2)}, u32[]{:S(2)}) async-start(bf16[16,32,896]{2,1,0:T(8,128)(2,1)} %bitcast.9), calls=%async_computation.3 | async-start | bytes 1835008 | tf_op jit(solution)/shard_map/all_to_all | solution.py:105
  371.2 2.8 gather_fusion.4
  374.0 0.1 reshape.299
  374.1 0.7 copy.29
  374.8 32.5 %reduce-scatter.11.cloned.1.call-done = bf16[1,1792,256]{2,1,0:T(8,128)(2,1)} async-done(((bf16[1,7168,256]{2,1,0:T(8,128)(2,1)}), bf16[1,1792,256]{2,1,0:T(8,128)(2,1)}) %reduce-scatter.11.cloned.1.call-update) | async-done | bytes 917520 | tf_op jit(solution)/shard_map/reduce_scatter | solution.py:133
  407.3 2.5 convert_element_type.141
  409.9 41.9 %reduce-scatter.7.cloned.1.call-done = bf16[1,1792,256]{2,1,0:T(8,128)(2,1)} async-done(((bf16[1,7168,256]{2,1,0:T(8,128)(2,1)}), bf16[1,1792,256]{2,1,0:T(8,128)(2,1)}) %reduce-scatter.7.cloned.1.call-update) | async-done | bytes 917520 | tf_op jit(solution)/shard_map/reduce_scatter | solution.py:127
  451.7 2.5 convert_element_type.132
  454.3 42.1 %reduce-scatter.9.cloned.1.call-done = bf16[1,1792,256]{2,1,0:T(8,128)(2,1)} async-done(((bf16[1,7168,256]{2,1,0:T(8,128)(2,1)}), bf16[1,1792,256]{2,1,0:T(8,128)(2,1)}) %reduce-scatter.9.cloned.1.call-update) | async-done | bytes 917520 | tf_op jit(solution)/shard_map/reduce_scatter | solution.py:130
  496.4 2.5 convert_element_type.135
  499.0 0.2 bitcast_convert_fusion
  499.2 1.9 gather_fusion.3
  501.1 0.8 reshape.298
  501.9 2.5 reduce_sum.33
  (36 shorter events, 0.7 us)
Async XLA Ops:
  7.2 211.1 %all-gather.8.cloned.1.call-start = ((), (), s32[]{:S(2)}) async-start(), calls=%async_computation.11 | async-start | bytes 4587520 | tf_op jit(solution)/shard_map/all_gather | solution.py:76
  36.4 80.3 %all-to-all-start.2 = ((bf16[16,32,3584]{2,1,0:T(8,128)(2,1)}), bf16[16,32,3584]{2,1,0:T(8,128)(2,1)}, u32[]{:S(2)}, u32[]{:S(2)}) async-start(bf16[16,32,3584]{2,1,0:T(8,128)(2,1)} %get-tuple-element.30), calls=%async_computation.2 | async-start | bytes 7340032 | tf_op jit(solution)/shard_map/all_to_all | solution.py:48
  45.3 179.2 %all-gather.6.cloned.1.call-start = ((), (), s32[]{:S(2)}) async-start(), calls=%async_computation.10 | async-start | bytes 4587520 | tf_op jit(solution)/shard_map/all_gather | solution.py:77
  116.7 90.4 %collective-permute-start.1 = (bf16[16,32,3584]{2,1,0:T(8,128)(2,1)}, bf16[16,32,3584]{2,1,0:T(8,128)(2,1)}, u32[]{:S(2)}, u32[]{:S(2)}) collective-permute-start(bf16[16,32,3584]{2,1,0:T(8,128)(2,1)} %all-to-all-done.2), channel_id=1, source_target_pairs={{0,1},{1,0},{2,3},{3,2},{4,5},{5,4},{6,7},{7,6},{8,9},{9,8},{10,11... | collective-permute-start | bytes 11010056 | tf_op jit(solution)/shard_map/ppermute | solution.py:54
  130.1 70.3 %all-to-all-start.1 = ((bf16[16,32,3584]{2,1,0:T(8,128)(2,1)}), bf16[16,32,3584]{2,1,0:T(8,128)(2,1)}, u32[]{:S(2)}, u32[]{:S(2)}) async-start(bf16[16,32,3584]{2,1,0:T(8,128)(2,1)} %get-tuple-element.29), calls=%async_computation.1 | async-start | bytes 7340032 | tf_op jit(solution)/shard_map/all_to_all | solution.py:49
  134.6 107.4 %all-gather.4.cloned.1.call-start = ((), (), s32[]{:S(2)}) async-start(), calls=%async_computation.9 | async-start | bytes 4587520 | tf_op jit(solution)/shard_map/all_gather | solution.py:78
  135.4 223.5 %reduce-scatter.13.cloned.1.call-start = ((), (), s32[]{:S(2)}) async-start(), calls=%async_computation.15 | async-start | bytes 8257536
  200.5 30.3 %collective-permute-start = (bf16[16,32,3584]{2,1,0:T(8,128)(2,1)}, bf16[16,32,3584]{2,1,0:T(8,128)(2,1)}, u32[]{:S(2)}, u32[]{:S(2)}) collective-permute-start(bf16[16,32,3584]{2,1,0:T(8,128)(2,1)} %all-to-all-done.1), channel_id=1, source_target_pairs={{0,1},{1,0},{2,3},{3,2},{4,5},{5,4},{6,7},{7,6},{8,9},{9,8},{10,11... | collective-permute-start | bytes 11010056 | tf_op jit(solution)/shard_map/ppermute | solution.py:54
  242.1 6.6 %copy-start.1 = (bf16[1,7168,256]{2,1,0:T(8,128)(2,1)S(1)}, bf16[1,7168,256]{2,1,0:T(8,128)(2,1)}, u32[]{:S(2)}) copy-start(bf16[1,7168,256]{2,1,0:T(8,128)(2,1)} %all-gather.8.cloned.1.call-done) | copy-start | bytes 11010052
  248.7 7.4 %copy-start = (bf16[1,7168,256]{2,1,0:T(8,128)(2,1)S(1)}, bf16[1,7168,256]{2,1,0:T(8,128)(2,1)}, u32[]{:S(2)}) copy-start(bf16[1,7168,256]{2,1,0:T(8,128)(2,1)} %all-gather.6.cloned.1.call-done) | copy-start | bytes 11010052
  308.4 98.9 %reduce-scatter.11.cloned.1.call-start = ((), (), s32[]{:S(2)}) async-start(), calls=%async_computation.14 | async-start | bytes 4587520 | tf_op jit(solution)/shard_map/reduce_scatter | solution.py:133
  316.5 135.2 %reduce-scatter.7.cloned.1.call-start = ((), (), s32[]{:S(2)}) async-start(), calls=%async_computation.12 | async-start | bytes 4587520 | tf_op jit(solution)/shard_map/reduce_scatter | solution.py:127
  323.7 172.7 %reduce-scatter.9.cloned.1.call-start = ((), (), s32[]{:S(2)}) async-start(), calls=%async_computation.13 | async-start | bytes 4587520 | tf_op jit(solution)/shard_map/reduce_scatter | solution.py:130
  355.1 9.9 %all-to-all-start.4 = ((bf16[16,1,32]{2,1,0:T(2,128)(2,1)}), bf16[16,1,32]{2,1,0:T(2,128)(2,1)S(1)}, u32[]{:S(2)}, u32[]{:S(2)}) async-start(bf16[16,1,32]{2,1,0:T(2,128)(2,1)} %convert_element_type.144), calls=%async_computation.4 | async-start | bytes 16384 | tf_op jit(solution)/shard_map/all_to_all | solution.py:112
  365.1 133.9 %all-to-all-start.3 = ((bf16[16,32,896]{2,1,0:T(8,128)(2,1)}), bf16[16,32,896]{2,1,0:T(8,128)(2,1)S(1)}, u32[]{:S(2)}, u32[]{:S(2)}) async-start(bf16[16,32,896]{2,1,0:T(8,128)(2,1)} %bitcast.9), calls=%async_computation.3 | async-start | bytes 1835008 | tf_op jit(solution)/shard_map/all_to_all | solution.py:105
Sparse Core Ops, SparseCore 0:
  9.7 68.7 all-gather.7
  80.2 55.4 all-gather.5
  137.3 70.2 all-gather.3
  308.6 43.6 reduce-scatter.12
  354.5 52.7 reduce-scatter.10
  409.6 42.1 reduce-scatter.6
  454.2 42.2 reduce-scatter.8
where the time goes:
time: 519 us; the launch traced here: 512 us
  waiting for transfers between devices  255 us (49%)
  local copies, waits for them, and re-layouts  73.9 us (14%)
  matrix products  59.3 us (11%)
  other arithmetic  42 us (8%)
  blocking collectives  35 us (7%)
  starting transfers between devices  31.7 us (6%)
  between operations  14.6 us (3%)
    all_to_all x1, waiting for transfers between devices, shards(): lax.all_to_all(in_send, ('expert', 'seq'), split_axis=0, concat_axis=0, t...  70.6 us
    all_to_all x1, waiting for transfers between devices, shards(): lax.all_to_all(out_send, ('expert', 'seq'), split_axis=0, concat_axis=0,...  64.9 us
    unnamed x11, local copies, waits for them, and re-layouts  49.6 us
    reduce_scatter x1, waiting for transfers between devices, shards(): lax.psum_scatter(up_part.astype(jnp.bfloat16), 'seq', scatter_dimension=1...  42.1 us
    reduce_scatter x1, waiting for transfers between devices, shards(): lax.psum_scatter(gate_part.astype(jnp.bfloat16), 'seq', scatter_dimension...  41.9 us
    reduce_scatter x1, waiting for transfers between devices, shards(): lax.psum_scatter(down_part.astype(jnp.bfloat16), 'seq', scatter_dimension...  32.5 us
    psum x1, blocking collectives, shards(): route_scores = lax.psum(partial_scores, ('tx', 'core'))  23.5 us
    all_to_all x1, blocking collectives, shards(): lax.all_to_all(weight_send, ('expert', 'seq'), split_axis=0, concat_axis=...  11.5 us
  transfers between devices with their start and end apart: 13, of which 6 were waited for; matrix products, arithmetic and copies ran while one was open for 20% of the time, Pallas kernels for 0%

commit v1 on v0

--- a/solution.py
+++ b/solution.py
@@ -97,7 +97,7 @@
     input_terms = input_terms + jnp.einsum(
         "emf,edf->emd", up_grad, up_full, preferred_element_type=jnp.float32
     )
-    route_scores = lax.psum(partial_scores, ("tx", "core"))
+    route_scores = lax.psum(lax.psum(partial_scores, "tx"), "core")
     input_shards = lax.psum_scatter(
         input_terms.astype(jnp.bfloat16), ("tx", "core"), scatter_dimension=2, tiled=True
     ).astype(jnp.float32)

time: 519 us -> 519 us (level)
  blocking collectives: 35 us -> 25.6 us
  waiting for transfers between devices: 255 us -> 264 us
    psum x1 -> x2, blocking collectives: 23.5 us -> 14.1 us  [shards(): route_scores = lax.psum(lax.psum(partial_scores, 'tx'), 'core')]
    reduce_scatter x1, waiting for transfers between devices: 32.5 us -> 39.1 us  [shards(): lax.psum_scatter(down_part.astype(jnp.bfloat16), 'seq', scatter_dimension...]
where the time goes in v1:
time: 519 us; the launch traced here: 512 us
  waiting for transfers between devices  264 us (51%)
  local copies, waits for them, and re-layouts  73.9 us (14%)
  matrix products  59.3 us (11%)
  other arithmetic  42 us (8%)
  starting transfers between devices  32.5 us (6%)
  blocking collectives  25.6 us (5%)
  between operations  14.6 us (3%)
    all_to_all x1, waiting for transfers between devices, shards(): lax.all_to_all(in_send, ('expert', 'seq'), split_axis=0, concat_axis=0, t...  70.6 us
    all_to_all x1, waiting for transfers between devices, shards(): lax.all_to_all(out_send, ('expert', 'seq'), split_axis=0, concat_axis=0,...  64.9 us
    unnamed x11, local copies, waits for them, and re-layouts  49.6 us
    reduce_scatter x1, waiting for transfers between devices, shards(): lax.psum_scatter(up_part.astype(jnp.bfloat16), 'seq', scatter_dimension=1...  42.1 us
    reduce_scatter x1, waiting for transfers between devices, shards(): lax.psum_scatter(gate_part.astype(jnp.bfloat16), 'seq', scatter_dimension...  42 us
    reduce_scatter x1, waiting for transfers between devices, shards(): lax.psum_scatter(down_part.astype(jnp.bfloat16), 'seq', scatter_dimension...  39.1 us
    psum x2, blocking collectives, shards(): route_scores = lax.psum(lax.psum(partial_scores, 'tx'), 'core')  14.1 us
    all_to_all x1, blocking collectives, shards(): lax.all_to_all(weight_send, ('expert', 'seq'), split_axis=0, concat_axis=...  11.5 us
  transfers between devices with their start and end apart: 13, of which 6 were waited for; matrix products, arithmetic and copies ran while one was open for 20% of the time, Pallas kernels for 0%

profile of v1, /device:TPU:1, one launch (start us, length us, event | category | flops | bytes accessed | tf_op | source)
XLA Modules:
  0.0 511.5 jit_solution(17637828552959129799)
XLA Ops:
  7.2 0.7 all-gather.8.cloned.1.call-update
  7.9 0.8 copy.24
  8.7 0.1 eq.38
  8.8 0.1 eq.34
  9.0 0.8 copy.26
  9.8 0.2 reshape.290
  10.0 0.7 broadcast_multiply_fusion.2
  10.7 0.1 copy.23
  10.8 0.1 mul.119
  11.0 1.2 reduce-window.6
  12.2 0.2 slice_reduce_fusion
  12.4 0.2 reduce-window.9
  12.7 2.9 scatter_custom_fusion
  15.7 3.5 gather_fusion
  19.2 0.1 reshape.301
  19.3 1.9 constant_dynamic-slice_fusion
  21.2 4.2 gather_fusion.2
  25.4 4.2 gather_fusion.1
  29.6 6.8 %broadcast_multiply_fusion.1 = (bf16[16,32,3584]{2,1,0:T(8,128)(2,1)}, bf16[16,32,3584]{2,1,0:T(8,128)(2,1)}) fusion(bf16[16,32,3584]{2,1,0:T(8,128)(2,1)} %bitcast.74, bf16[16,32]{1,0:T(8,128)(2,1)S(1)} %reshape.301, bf16[16,32,3584]{2,1,0:T(8,128)(2,1)} %bitcast.73), kind=kLoop, calls=%fused_computation.34 | loop fusion | flops 3670016 | bytes 14681088 | tf_op jit(solution)/shard_map/mul | solution.py:46
  36.4 8.9 %all-to-all-start.2 = ((bf16[16,32,3584]{2,1,0:T(8,128)(2,1)}), bf16[16,32,3584]{2,1,0:T(8,128)(2,1)}, u32[]{:S(2)}, u32[]{:S(2)}) async-start(bf16[16,32,3584]{2,1,0:T(8,128)(2,1)} %get-tuple-element.30), calls=%async_computation.2 | async-start | bytes 7340032 | tf_op jit(solution)/shard_map/all_to_all | solution.py:48
  45.3 0.7 all-gather.6.cloned.1.call-update
  46.0 70.6 %all-to-all-done.2 = bf16[16,32,3584]{2,1,0:T(8,128)(2,1)} async-done(((bf16[16,32,3584]{2,1,0:T(8,128)(2,1)}), bf16[16,32,3584]{2,1,0:T(8,128)(2,1)}, u32[]{:S(2)}, u32[]{:S(2)}) %all-to-all-start.2) | async-done | bytes 3670048 | tf_op jit(solution)/shard_map/all_to_all | solution.py:48
  116.7 1.8 collective-permute-start.1
  118.5 0.1 all_to_all.25
  118.6 11.5 %all_to_all.31 = bf16[16,1,32]{2,1,0:T(2,128)(2,1)S(1)} all-to-all(bf16[16,1,32]{2,1,0:T(2,128)(2,1)S(1)} %all_to_all.25), channel_id=1, replica_groups=mesh['expert'=4,'seq'=4,'tx'=4,'core'=2] {'expert','seq'}, dimensions={0} | all-to-all | bytes 2048 | tf_op jit(solution)/shard_map/all_to_all | solution.py:50
  130.1 4.5 all-to-all-start.1
  134.7 0.7 all-gather.4.cloned.1.call-update
  135.5 64.9 %all-to-all-done.1 = bf16[16,32,3584]{2,1,0:T(8,128)(2,1)} async-done(((bf16[16,32,3584]{2,1,0:T(8,128)(2,1)}), bf16[16,32,3584]{2,1,0:T(8,128)(2,1)}, u32[]{:S(2)}, u32[]{:S(2)}) %all-to-all-start.1) | async-done | bytes 3670048 | tf_op jit(solution)/shard_map/all_to_all | solution.py:49
  200.5 6.6 %collective-permute-start = (bf16[16,32,3584]{2,1,0:T(8,128)(2,1)}, bf16[16,32,3584]{2,1,0:T(8,128)(2,1)}, u32[]{:S(2)}, u32[]{:S(2)}) collective-permute-start(bf16[16,32,3584]{2,1,0:T(8,128)(2,1)} %all-to-all-done.1), channel_id=1, source_target_pairs={{0,1},{1,0},{2,3},{3,2},{4,5},{5,4},{6,7},{7,6},{8,9},{9,8},{10,11... | collective-permute-start | bytes 11010056 | tf_op jit(solution)/shard_map/ppermute | solution.py:54
  207.0 5.4 %broadcast_select_fusion.1 = (bf16[16,32,3584]{2,1,0:T(8,128)(2,1)S(1)}, bf16[16,32,3584]{2,1,0:T(8,128)(2,1)}) fusion(bf16[16,32,3584]{2,1,0:T(8,128)(2,1)} %all-to-all-done.2, bf16[16,32,3584]{2,1,0:T(8,128)(2,1)} %collective-permute-done.1, pred[]{:T(512)S(6)} %eq.42), kind=kLoop, calls=%fused_computation.29 | loop fusion | flops 3670016 | bytes 14680065 | tf_op jit(solution)/shard_map/jit(_where)/select_n | solution.py:55
  212.5 5.8 %pad_maximum_fusion.1 = bf16[16,32,7168]{2,1,0:T(8,128)(2,1)} fusion(bf16[16,32,3584]{2,1,0:T(8,128)(2,1)} %get-tuple-element.25, bf16[16,32,3584]{2,1,0:T(8,128)(2,1)S(1)} %get-tuple-element.24), kind=kLoop, calls=%fused_computation.16 | loop fusion | flops 14680064 | bytes 14680064 | tf_op jit(solution)/shard_map/concatenate | solution.py:57
  218.2 6.2 %fusion.7 = f32[512,256]{0,1:T(8,128)S(1)} fusion(bf16[512,7168]{1,0:T(8,128)(2,1)} %bitcast.67, bf16[1,7168,256]{2,1,0:T(8,128)(2,1)} %all-gather.8.cloned.1.call-done), kind=kOutput, calls=%fused_computation.21 | convolution fusion | flops 1879048192 | bytes 11534336 | tf_op jit(solution)/shard_map/emd,edf->emf/dot_general | solution.py:80
  224.5 6.2 %fusion.10 = f32[512,256]{0,1:T(8,128)S(1)} fusion(bf16[512,7168]{1,0:T(8,128)(2,1)} %bitcast.68, bf16[1,7168,256]{2,1,0:T(8,128)(2,1)} %all-gather.6.cloned.1.call-done), kind=kOutput, calls=%fused_computation.24 | convolution fusion | flops 1879048192 | bytes 11534336 | tf_op jit(solution)/shard_map/emd,edf->emf/dot_general | solution.py:81
  230.7 5.6 %broadcast_select_fusion.3 = (bf16[16,32,3584]{2,1,0:T(8,128)(2,1)S(1)}, bf16[16,32,3584]{2,1,0:T(8,128)(2,1)}) fusion(bf16[16,32,3584]{2,1,0:T(8,128)(2,1)} %all-to-all-done.1, bf16[16,32,3584]{2,1,0:T(8,128)(2,1)} %collective-permute-done, pred[]{:T(512)S(6)} %eq.42), kind=kLoop, calls=%fused_computation.31 | loop fusion | flops 3670016 | bytes 14680065 | tf_op jit(solution)/shard_map/jit(_where)/select_n | solution.py:55
  236.3 5.8 %pad_maximum_fusion = bf16[16,32,7168]{2,1,0:T(8,128)(2,1)} fusion(bf16[16,32,3584]{2,1,0:T(8,128)(2,1)} %get-tuple-element.23, bf16[16,32,3584]{2,1,0:T(8,128)(2,1)S(1)} %get-tuple-element.22), kind=kLoop, calls=%fused_computation.15 | loop fusion | flops 14680064 | bytes 14680064 | tf_op jit(solution)/shard_map/concatenate | solution.py:57
  242.1 6.6 %multiply_reduce_fusion = (f32[512]{0:T(512)S(1)}, bf16[512,256]{0,1:T(8,128)(2,1)S(1)}, bf16[512,256]{0,1:T(8,128)(2,1)S(1)}) fusion(f32[512,256]{0,1:T(8,128)S(1)} %fusion.10, f32[512,256]{0,1:T(8,128)S(1)} %fusion.7, f32[512]{0:T(512)S(1)} %reshape.300, bf16[512,7168]{1,0:T(8,128)(2,1)} %bitcast.75, bf16[1,7168,256]{2,1,0:T(8,128)(2,1)} %all-gather.4.cloned.1.call-done), kind=kOutput, calls=%fused_computation.36 | convolution fusion | flops 1881275904 | bytes 12587008 | tf_op jit(solution)/shard_map/emd,edf->emf/dot_general | solution.py:86
  248.7 7.3 %fusion.5 = f32[512,7168]{1,0:T(8,128)} fusion(bf16[512,256]{0,1:T(8,128)(2,1)S(1)} %get-tuple-element.27, bf16[1,7168,256]{2,1,0:T(8,128)(2,1)S(1)} %copy-done.1), kind=kOutput, calls=%fused_computation.19 | convolution fusion | flops 1879048192 | bytes 18612224 | tf_op jit(solution)/shard_map/emf,edf->emd/dot_general | solution.py:94
  256.0 10.6 %fusion = bf16[1,512,7168]{2,1,0:T(8,128)(2,1)} fusion(f32[512,7168]{1,0:T(8,128)} %fusion.5, bf16[512,256]{0,1:T(8,128)(2,1)S(1)} %get-tuple-element.28, bf16[1,7168,256]{2,1,0:T(8,128)(2,1)S(1)} %copy-done), kind=kOutput, calls=%fused_computation.8 | convolution fusion | flops 1886388224 | bytes 25952256 | tf_op jit(solution)/shard_map/emf,edf->emd/dot_general | solution.py:97
  266.6 31.4 %copy.30 = bf16[1,512,7168]{1,0,2:T(2,128)(2,1)} copy(bf16[1,512,7168]{2,1,0:T(8,128)(2,1)} %fusion) | data formatting | bytes 14680064
  298.1 10.3 %copy.36 = bf16[7168,1,512]{2,0,1:T(8,128)(2,1)} copy(bf16[7168,1,512]{2,1,0:T(2,128)(2,1)} %bitcast.71) | data formatting | bytes 14680064
  308.5 8.0 %fusion.3 = bf16[1,7168,256]{2,1,0:T(8,128)(2,1)} fusion(bf16[512,7168]{1,0:T(8,128)(2,1)} %bitcast.76, f32[512]{0:T(512)S(1)} %reshape.300, f32[512,256]{0,1:T(8,128)S(1)} %fusion.10, f32[512,256]{0,1:T(8,128)S(1)} %fusion.7), kind=kOutput, calls=%fused_computation.14 | convolution fusion | flops 1892679680 | bytes 12060672 | tf_op jit(solution)/shard_map/emd,emf->edf/dot_general | solution.py:125
  316.6 7.1 %fusion.1 = bf16[1,7168,256]{2,1,0:T(8,128)(2,1)} fusion(bf16[512,7168]{1,0:T(8,128)(2,1)} %bitcast.69, bf16[512,256]{0,1:T(8,128)(2,1)S(1)} %get-tuple-element.27), kind=kOutput, calls=%fused_computation.12 | convolution fusion | flops 1880883200 | bytes 11272192 | tf_op jit(solution)/shard_map/emd,emf->edf/dot_general | solution.py:123
  323.8 7.2 %fusion.2 = bf16[1,7168,256]{2,1,0:T(8,128)(2,1)} fusion(bf16[512,7168]{1,0:T(8,128)(2,1)} %bitcast.70, bf16[512,256]{0,1:T(8,128)(2,1)S(1)} %get-tuple-element.28), kind=kOutput, calls=%fused_computation.13 | convolution fusion | flops 1880883200 | bytes 11272192 | tf_op jit(solution)/shard_map/emd,emf->edf/dot_general | solution.py:124
  330.9 9.4 %psum.14 = f32[1,512]{1,0:T(1,128)S(1)} all-reduce(f32[1,512]{1,0:T(1,128)S(1)} %bitcast.78), channel_id=1, replica_groups=mesh['expert'=4,'seq'=4,'tx'=4,'core'=2] {'tx'}, use_global_device_ids=true, to_apply=%region_7.8 | all-reduce | flops 512 | bytes 4096 | tf_op jit(solution)/shard_map/psum | solution.py:100
  340.3 4.7 psum.15
  345.1 0.7 convert_element_type.144
  345.8 3.7 all-to-all-start.4
  349.4 2.7 reduce-scatter.13.cloned.1.call-done
  352.1 2.1 reshape_bitcast_fusion
  354.3 3.4 copy.31
  357.7 6.7 %all-to-all-start.3 = ((bf16[16,32,896]{2,1,0:T(8,128)(2,1)}), bf16[16,32,896]{2,1,0:T(8,128)(2,1)S(1)}, u32[]{:S(2)}, u32[]{:S(2)}) async-start(bf16[16,32,896]{2,1,0:T(8,128)(2,1)} %bitcast.9), calls=%async_computation.3 | async-start | bytes 1835008 | tf_op jit(solution)/shard_map/all_to_all | solution.py:105
  364.5 2.8 gather_fusion.4
  367.3 0.1 reshape.299
  367.4 0.7 copy.29
  368.1 39.1 %reduce-scatter.11.cloned.1.call-done = bf16[1,1792,256]{2,1,0:T(8,128)(2,1)} async-done(((bf16[1,7168,256]{2,1,0:T(8,128)(2,1)}), bf16[1,1792,256]{2,1,0:T(8,128)(2,1)}) %reduce-scatter.11.cloned.1.call-update) | async-done | bytes 917520 | tf_op jit(solution)/shard_map/reduce_scatter | solution.py:133
  407.2 2.5 convert_element_type.141
  409.7 42.0 %reduce-scatter.7.cloned.1.call-done = bf16[1,1792,256]{2,1,0:T(8,128)(2,1)} async-done(((bf16[1,7168,256]{2,1,0:T(8,128)(2,1)}), bf16[1,1792,256]{2,1,0:T(8,128)(2,1)}) %reduce-scatter.7.cloned.1.call-update) | async-done | bytes 917520 | tf_op jit(solution)/shard_map/reduce_scatter | solution.py:127
  451.7 2.5 convert_element_type.132
  454.3 42.1 %reduce-scatter.9.cloned.1.call-done = bf16[1,1792,256]{2,1,0:T(8,128)(2,1)} async-done(((bf16[1,7168,256]{2,1,0:T(8,128)(2,1)}), bf16[1,1792,256]{2,1,0:T(8,128)(2,1)}) %reduce-scatter.9.cloned.1.call-update) | async-done | bytes 917520 | tf_op jit(solution)/shard_map/reduce_scatter | solution.py:130
  496.4 2.5 convert_element_type.135
  499.0 0.2 bitcast_convert_fusion
  499.2 1.9 gather_fusion.3
  501.1 0.8 reshape.298
  501.9 2.5 reduce_sum.33
  (37 shorter events, 0.8 us)
Async XLA Ops:
  7.2 211.1 %all-gather.8.cloned.1.call-start = ((), (), s32[]{:S(2)}) async-start(), calls=%async_computation.11 | async-start | bytes 4587520 | tf_op jit(solution)/shard_map/all_gather | solution.py:76
  36.4 80.3 %all-to-all-start.2 = ((bf16[16,32,3584]{2,1,0:T(8,128)(2,1)}), bf16[16,32,3584]{2,1,0:T(8,128)(2,1)}, u32[]{:S(2)}, u32[]{:S(2)}) async-start(bf16[16,32,3584]{2,1,0:T(8,128)(2,1)} %get-tuple-element.30), calls=%async_computation.2 | async-start | bytes 7340032 | tf_op jit(solution)/shard_map/all_to_all | solution.py:48
  45.3 179.2 %all-gather.6.cloned.1.call-start = ((), (), s32[]{:S(2)}) async-start(), calls=%async_computation.10 | async-start | bytes 4587520 | tf_op jit(solution)/shard_map/all_gather | solution.py:77
  116.7 90.4 %collective-permute-start.1 = (bf16[16,32,3584]{2,1,0:T(8,128)(2,1)}, bf16[16,32,3584]{2,1,0:T(8,128)(2,1)}, u32[]{:S(2)}, u32[]{:S(2)}) collective-permute-start(bf16[16,32,3584]{2,1,0:T(8,128)(2,1)} %all-to-all-done.2), channel_id=1, source_target_pairs={{0,1},{1,0},{2,3},{3,2},{4,5},{5,4},{6,7},{7,6},{8,9},{9,8},{10,11... | collective-permute-start | bytes 11010056 | tf_op jit(solution)/shard_map/ppermute | solution.py:54
  130.1 70.3 %all-to-all-start.1 = ((bf16[16,32,3584]{2,1,0:T(8,128)(2,1)}), bf16[16,32,3584]{2,1,0:T(8,128)(2,1)}, u32[]{:S(2)}, u32[]{:S(2)}) async-start(bf16[16,32,3584]{2,1,0:T(8,128)(2,1)} %get-tuple-element.29), calls=%async_computation.1 | async-start | bytes 7340032 | tf_op jit(solution)/shard_map/all_to_all | solution.py:49
  134.6 107.4 %all-gather.4.cloned.1.call-start = ((), (), s32[]{:S(2)}) async-start(), calls=%async_computation.9 | async-start | bytes 4587520 | tf_op jit(solution)/shard_map/all_gather | solution.py:78
  135.4 216.8 %reduce-scatter.13.cloned.1.call-start = ((), (), s32[]{:S(2)}) async-start(), calls=%async_computation.15 | async-start | bytes 8257536
  200.5 30.3 %collective-permute-start = (bf16[16,32,3584]{2,1,0:T(8,128)(2,1)}, bf16[16,32,3584]{2,1,0:T(8,128)(2,1)}, u32[]{:S(2)}, u32[]{:S(2)}) collective-permute-start(bf16[16,32,3584]{2,1,0:T(8,128)(2,1)} %all-to-all-done.1), channel_id=1, source_target_pairs={{0,1},{1,0},{2,3},{3,2},{4,5},{5,4},{6,7},{7,6},{8,9},{9,8},{10,11... | collective-permute-start | bytes 11010056 | tf_op jit(solution)/shard_map/ppermute | solution.py:54
  242.1 6.6 %copy-start.1 = (bf16[1,7168,256]{2,1,0:T(8,128)(2,1)S(1)}, bf16[1,7168,256]{2,1,0:T(8,128)(2,1)}, u32[]{:S(2)}) copy-start(bf16[1,7168,256]{2,1,0:T(8,128)(2,1)} %all-gather.8.cloned.1.call-done) | copy-start | bytes 11010052
  248.7 7.4 %copy-start = (bf16[1,7168,256]{2,1,0:T(8,128)(2,1)S(1)}, bf16[1,7168,256]{2,1,0:T(8,128)(2,1)}, u32[]{:S(2)}) copy-start(bf16[1,7168,256]{2,1,0:T(8,128)(2,1)} %all-gather.6.cloned.1.call-done) | copy-start | bytes 11010052
  308.4 98.8 %reduce-scatter.11.cloned.1.call-start = ((), (), s32[]{:S(2)}) async-start(), calls=%async_computation.14 | async-start | bytes 4587520 | tf_op jit(solution)/shard_map/reduce_scatter | solution.py:133
  316.5 135.2 %reduce-scatter.7.cloned.1.call-start = ((), (), s32[]{:S(2)}) async-start(), calls=%async_computation.12 | async-start | bytes 4587520 | tf_op jit(solution)/shard_map/reduce_scatter | solution.py:127
  323.7 172.7 %reduce-scatter.9.cloned.1.call-start = ((), (), s32[]{:S(2)}) async-start(), calls=%async_computation.13 | async-start | bytes 4587520 | tf_op jit(solution)/shard_map/reduce_scatter | solution.py:130
  345.8 11.9 %all-to-all-start.4 = ((bf16[16,1,32]{2,1,0:T(2,128)(2,1)}), bf16[16,1,32]{2,1,0:T(2,128)(2,1)S(1)}, u32[]{:S(2)}, u32[]{:S(2)}) async-start(bf16[16,1,32]{2,1,0:T(2,128)(2,1)} %convert_element_type.144), calls=%async_computation.4 | async-start | bytes 16384 | tf_op jit(solution)/shard_map/all_to_all | solution.py:112
  357.7 141.3 %all-to-all-start.3 = ((bf16[16,32,896]{2,1,0:T(8,128)(2,1)}), bf16[16,32,896]{2,1,0:T(8,128)(2,1)S(1)}, u32[]{:S(2)}, u32[]{:S(2)}) async-start(bf16[16,32,896]{2,1,0:T(8,128)(2,1)} %bitcast.9), calls=%async_computation.3 | async-start | bytes 1835008 | tf_op jit(solution)/shard_map/all_to_all | solution.py:105
Sparse Core Ops, SparseCore 0:
  9.7 68.7 all-gather.7
  80.2 55.4 all-gather.5
  137.3 70.2 all-gather.3
  308.6 43.5 reduce-scatter.12
  354.4 52.7 reduce-scatter.10
  409.5 42.2 reduce-scatter.6
  454.2 42.2 reduce-scatter.8
